TPU v7x, 32 devices: a whole 2x2x4 slice. The times are simulated.
32 devices in a mesh: seq: 16 (over z, y, core), head: 2 (over x).
Axes of the slice: x: 2, y: 2, z: 4, core: 2. Of those that a mesh axis runs over, the one named last changes fastest.
Arguments:
- qkv: bfloat16 [3, 2048, 1024], P(None, ('seq', 'head')), may hold values from -128 to 128
- token_rate: float32 [2048, 2], P('seq', 'head'), may hold values from 0.1 to 1
- head_rate: float32 [2], P('head'), may hold values from 0.5 to 2
- fast_state: float32 [3, 2, 512, 512], P(None, 'head', 'seq'), may hold values from -0.25 to 0.25
Outputs:
- combined: bfloat16 [2048, 1024], P(('seq', 'head'))
- new_state: float32 [3, 2, 512, 512], P(None, 'head', 'seq')
All inputs are finite; a program needn't handle non-finite values.
Results may differ from a plain program's by a relative error of at most 0.017.
Values may be sent and summed in bfloat16 or wider, within the bound.
A program may use at most 64 MiB of HBM per device.

v0:
```python
import jax
import jax.numpy as jnp
from jax import lax
from jax.sharding import PartitionSpec as P

WINDOW = 1024
NS_STEPS = 2
ns_first = 3.4445
ns_second = -4.775
ns_third = 2.0315
rms_eps = 1e-06
norm_eps = 1e-07
precise = lax.Precision.HIGHEST


def from_behind(block, axis, distance):
    devices = range(lax.axis_size(axis))
    route = [(i - distance, i) for i in devices if i - distance in devices]
    return lax.ppermute(block, axis, route)


def rms_scaled(values):
    return values * lax.rsqrt(jnp.mean(values * values, axis=-1, keepdims=True) + rms_eps)


def contract_last(left_side, right_side):
    return lax.dot_general(
        left_side, right_side, (((1,), (1,)), ((), ())), preferred_element_type=jnp.float32
    )


def contract_first(left_side, right_side):
    return lax.dot_general(
        left_side, right_side, (((0,), (0,)), ((), ())), preferred_element_type=jnp.float32
    )


def head_gradient(key_norm, signal, weight_piece):
    gate_act = contract_last(key_norm, weight_piece[0])
    up_act = contract_last(key_norm, weight_piece[1])
    active = (jax.nn.silu(gate_act) * up_act).astype(jnp.bfloat16)
    back_grad = contract_last(signal, weight_piece[2])
    sigmoid_gate = jax.nn.sigmoid(gate_act)
    grad_gate = (
        back_grad * up_act * sigmoid_gate * (1.0 + gate_act * (1.0 - sigmoid_gate))
    ).astype(jnp.bfloat16)
    grad_up = (back_grad * jax.nn.silu(gate_act)).astype(jnp.bfloat16)
    return jnp.stack(
        [
            contract_first(grad_gate, key_norm),
            contract_first(grad_up, key_norm),
            contract_first(active, signal),
        ]
    )


def gram_times(gram_matrix, section_number, row_block):
    if section_number == 0:
        return jnp.einsum("mij,mjk->mik", row_block, gram_matrix, precision=precise)
    once_moved = gram_times(gram_matrix, section_number - 1, row_block)
    return poly_times(
        gram_matrix, section_number - 1, poly_times(gram_matrix, section_number - 1, once_moved)
    )


def poly_times(gram_matrix, section_number, row_block):
    moved_once = gram_times(gram_matrix, section_number, row_block)
    moved_twice = gram_times(gram_matrix, section_number, moved_once)
    return ns_first * row_block + ns_second * moved_once + ns_third * moved_twice


def shards(qkv, token_rate, head_rate, fast_state):
    grouped = lax.all_to_all(qkv, "head", split_axis=2, concat_axis=1, tiled=True)
    tok_rows = grouped.shape[1]
    head_dim = grouped.shape[2]
    seq_index = lax.axis_index("seq")
    state_rows = fast_state.shape[2]
    query_norm = rms_scaled(grouped[0].astype(jnp.float32)).astype(jnp.bfloat16)
    key_norm = rms_scaled(grouped[1].astype(jnp.float32)).astype(jnp.bfloat16)
    signal = (-token_rate * grouped[2].astype(jnp.float32)).astype(jnp.bfloat16)
    old_state = fast_state[:, 0]
    old_low = old_state.astype(jnp.bfloat16)
    partial_value = head_gradient(
        key_norm, signal, lax.all_gather(old_low, "seq", axis=1, tiled=True)
    )
    summed = lax.psum(partial_value, "seq")
    frob_norm = jnp.sqrt(jnp.sum(summed * summed, axis=(1, 2), keepdims=True))
    normalized = summed / (frob_norm + norm_eps)
    gram_matrix = jnp.einsum("mij,mkj->mik", normalized, normalized, precision=precise)
    hidden_units = gram_matrix.shape[1]
    selector = (
        jnp.arange(hidden_units, dtype=jnp.int32)[None, :]
        == seq_index * state_rows + jnp.arange(state_rows, dtype=jnp.int32)[:, None]
    ).astype(jnp.float32)
    row_block = jnp.broadcast_to(selector, (3, state_rows, hidden_units))
    for section_number in range(NS_STEPS - 1, -1, -1):
        row_block = poly_times(gram_matrix, section_number, row_block)
    final_rows = jnp.einsum("mij,mjk->mik", row_block, normalized, precision=precise)
    new_rows = old_state - head_rate[0] * final_rows
    weight_piece = lax.all_gather(new_rows.astype(jnp.bfloat16), "seq", axis=1, tiled=True)
    gate_act = contract_last(query_norm, weight_piece[0])
    up_act = contract_last(query_norm, weight_piece[1])
    active = (jax.nn.silu(gate_act) * up_act).astype(jnp.bfloat16)
    fast_out = jnp.dot(active, weight_piece[2], preferred_element_type=jnp.float32)
    key_value = grouped[1:3]
    reach_blocks = WINDOW // tok_rows
    earlier = [from_behind(key_value, "seq", distance) for distance in range(reach_blocks, 0, -1)]
    context = jnp.concatenate(earlier + [key_value], axis=1)
    scores = contract_last(grouped[0], context[0]) * head_dim ** (-0.5)
    query_pos = seq_index * tok_rows + jnp.arange(tok_rows, dtype=jnp.int32)[:, None]
    key_pos = (
        seq_index * tok_rows - WINDOW + jnp.arange(WINDOW + tok_rows, dtype=jnp.int32)[None, :]
    )
    visible = (key_pos <= query_pos) & (key_pos > query_pos - WINDOW) & (key_pos >= 0)
    scores = jnp.where(visible, scores, -jnp.inf)
    row_max = jnp.max(scores, axis=1, keepdims=True)
    exp_scores = jnp.exp(scores - row_max)
    weights = (exp_scores / jnp.sum(exp_scores, axis=1, keepdims=True)).astype(jnp.bfloat16)
    attention = jnp.dot(weights, context[1], preferred_element_type=jnp.float32)
    combined = (attention + fast_out).astype(jnp.bfloat16)
    tokens_back = lax.all_to_all(combined, "head", split_axis=0, concat_axis=1, tiled=True)
    return (tokens_back, new_rows[:, None])


def solution(mesh):
    return jax.shard_map(
        shards,
        mesh=mesh,
        in_specs=(
            P(None, ("seq", "head"), None),
            P("seq", "head"),
            P("head"),
            P(None, "head", "seq", None),
        ),
        out_specs=(P(("seq", "head"), None), P(None, "head", "seq", None)),
        check_vma=False,
    )
```

profile of v0, /device:TPU:16, one launch (start us, length us, event | category | flops | bytes accessed | tf_op | source)
XLA Modules:
  0.0 289.8 jit_solution(17737878514424476235)
XLA Ops:
  11.9 3.5 %all-to-all-start = ((bf16[2,2,49152]{2,1,0:T(2,128)(2,1)}), bf16[2,2,49152]{2,1,0:T(2,128)(2,1)S(1)}, u32[]{:S(2)}, u32[]{:S(2)}) async-start(bf16[2,2,49152]{2,1,0:T(2,128)(2,1)} %reshape.124), calls=%async_computation | async-start | bytes 786432 | tf_op jit(solution)/shard_map/all_to_all | solution.py:73
  15.5 6.7 %all-to-all-done = bf16[2,2,49152]{2,1,0:T(2,128)(2,1)S(1)} async-done(((bf16[2,2,49152]{2,1,0:T(2,128)(2,1)}), bf16[2,2,49152]{2,1,0:T(2,128)(2,1)S(1)}, u32[]{:S(2)}, u32[]{:S(2)}) %all-to-all-start) | async-done | bytes 393248 | tf_op jit(solution)/shard_map/all_to_all | solution.py:73
  24.0 25.6 %all-gather.3.cloned.1.call-done = bf16[3,512,512]{2,1,0:T(8,128)(2,1)} async-done(((bf16[3,32,512]{2,1,0:T(8,128)(2,1)}), bf16[3,512,512]{2,1,0:T(8,128)(2,1)}) %all-gather.3.cloned.1.call-update) | async-done | bytes 1572880 | tf_op jit(solution)/shard_map/all_gather | solution.py:84
  54.7 2.0 pad_maximum_fusion
  57.8 102.6 %all-reduce.2.cloned.1.call-done = f32[3,512,512]{2,1,0:T(8,128)} async-done(((f32[3,512,512]{2,1,0:T(8,128)}), f32[3,512,512]{2,1,0:T(8,128)}) %all-reduce.2.cloned.1.call-update) | async-done | bytes 3145744 | tf_op jit(solution)/shard_map/psum | solution.py:86
  160.3 2.5 multiply_reduce_fusion
  163.2 5.6 %fusion.15 = f32[3,512,512]{2,1,0:T(8,128)S(1)} fusion(f32[3,512,512]{2,1,0:T(8,128)S(1)} %copy-done, f32[3]{0:T(128)S(1)} %sqrt_add_fusion), kind=kOutput, calls=%fused_computation.33 | convolution fusion | flops 4832624640 | bytes 6291468 | tf_op jit(solution)/shard_map/mij,mkj->mik/dot_general | solution.py:89
  176.4 2.1 fusion.11
  190.0 2.1 fusion.6
  192.1 2.8 fusion.46
  196.3 1.9 collective-permute-start.1
  198.2 2.9 collective-permute-start.2
  201.1 1.9 collective-permute-start.3
  203.1 1.9 collective-permute-start.4
  205.0 2.3 collective-permute-done
  207.3 1.9 collective-permute-start.5
  209.2 12.2 %collective-permute-start.6 = (bf16[2,128,512]{2,1,0:T(8,128)(2,1)S(1)}, bf16[2,128,512]{2,1,0:T(8,128)(2,1)S(1)}, u32[]{:S(2)}, u32[]{:S(2)}) collective-permute-start(bf16[2,128,512]{2,1,0:T(8,128)(2,1)S(1)} %bitcast.119), channel_id=1, source_target_pairs={{0,4},{2,6},{4,8},{6,10},{8,12},{10,14},{12,16},{14,18},{16,20},{1... | collective-permute-start | bytes 786440 | tf_op jit(solution)/shard_map/ppermute | solution.py:19
  221.8 13.3 %collective-permute-start.7 = (bf16[2,128,512]{2,1,0:T(8,128)(2,1)S(1)}, bf16[2,128,512]{2,1,0:T(8,128)(2,1)S(1)}, u32[]{:S(2)}, u32[]{:S(2)}) collective-permute-start(bf16[2,128,512]{2,1,0:T(8,128)(2,1)S(1)} %bitcast.120), channel_id=1, source_target_pairs={{0,2},{2,4},{4,6},{6,8},{8,10},{10,12},{12,14},{14,16},{16,18},{18... | collective-permute-start | bytes 786440 | tf_op jit(solution)/shard_map/ppermute | solution.py:19
  235.2 8.6 %collective-permute-done.4 = bf16[2,128,512]{2,1,0:T(8,128)(2,1)S(1)} collective-permute-done((bf16[2,128,512]{2,1,0:T(8,128)(2,1)S(1)}, bf16[2,128,512]{2,1,0:T(8,128)(2,1)S(1)}, u32[]{:S(2)}, u32[]{:S(2)}) %collective-permute-start.4) | collective-permute-done | bytes 262176 | tf_op jit(solution)/shard_map/ppermute | solution.py:19
  243.9 2.9 collective-permute-done.5
  246.8 20.7 %collective-permute-done.6 = bf16[2,128,512]{2,1,0:T(8,128)(2,1)S(1)} collective-permute-done((bf16[2,128,512]{2,1,0:T(8,128)(2,1)S(1)}, bf16[2,128,512]{2,1,0:T(8,128)(2,1)S(1)}, u32[]{:S(2)}, u32[]{:S(2)}) %collective-permute-start.6) | collective-permute-done | bytes 262176 | tf_op jit(solution)/shard_map/ppermute | solution.py:19
  267.5 2.3 collective-permute-done.7
  271.9 2.4 fusion.14
  275.6 7.0 %all_to_all.34 = bf16[2,64,512]{2,1,0:T(8,128)(2,1)S(1)} all-to-all(bf16[2,64,512]{2,1,0:T(8,128)(2,1)S(1)} %bitcast.127), channel_id=1, replica_groups=mesh['seq'=16,'head'=2] {'head'}, dimensions={0} | all-to-all | bytes 262144 | tf_op jit(solution)/shard_map/all_to_all | solution.py:121
  (69 shorter events, 37.2 us)
Async XLA Ops:
  7.2 8.2 %copy-start.2 = (f32[128,1]{0,1:T(1,128)S(1)}, f32[128,1]{0,1:T(1,128)}, u32[]{:S(2)}) copy-start(f32[128,1]{0,1:T(1,128)} %param.5) | copy-start | bytes 1540
  7.2 42.5 %all-gather.3.cloned.1.call-start = ((), (), s32[]{:S(2)}) async-start(), calls=%async_computation.2 | async-start | bytes 1671168 | tf_op jit(solution)/shard_map/all_gather | solution.py:84
  11.9 10.3 %all-to-all-start = ((bf16[2,2,49152]{2,1,0:T(2,128)(2,1)}), bf16[2,2,49152]{2,1,0:T(2,128)(2,1)S(1)}, u32[]{:S(2)}, u32[]{:S(2)}) async-start(bf16[2,2,49152]{2,1,0:T(2,128)(2,1)} %reshape.124), calls=%async_computation | async-start | bytes 786432 | tf_op jit(solution)/shard_map/all_to_all | solution.py:73
  15.3 145.0 %all-reduce.2.cloned.1.call-start = ((), (), s32[]{:S(2)}) async-start(), calls=%async_computation.3 | async-start | bytes 6291456 | tf_op jit(solution)/shard_map/psum | solution.py:86
  56.7 213.8 %all-gather.5.cloned.1.call-start = ((), (), s32[]{:S(2)}) async-start(), calls=%async_computation.4 | async-start | bytes 1671168 | tf_op jit(solution)/shard_map/all_gather | solution.py:100
  160.3 2.8 copy-start
  188.1 4.1 %copy-start.1 = (f32[3,1,32,512]{3,2,1,0:T(8,128)S(1)}, f32[3,1,32,512]{3,2,1,0:T(8,128)}, u32[]{:S(2)}) copy-start(f32[3,1,32,512]{3,2,1,0:T(8,128)} %param.7) | copy-start | bytes 589828
  195.0 12.3 %collective-permute-start = (bf16[2,128,512]{2,1,0:T(8,128)(2,1)S(1)}, bf16[2,128,512]{2,1,0:T(8,128)(2,1)S(1)}, u32[]{:S(2)}, u32[]{:S(2)}) collective-permute-start(bf16[2,128,512]{2,1,0:T(8,128)(2,1)S(1)} %bitcast.113), channel_id=1, source_target_pairs={{0,16},{2,18},{4,20},{6,22},{8,24},{10,26},{12,28},{14,30},{1,17},... | collective-permute-start | bytes 786440 | tf_op jit(solution)/shard_map/ppermute | solution.py:19
  196.3 12.9 %collective-permute-start.1 = (bf16[2,128,512]{2,1,0:T(8,128)(2,1)S(1)}, bf16[2,128,512]{2,1,0:T(8,128)(2,1)S(1)}, u32[]{:S(2)}, u32[]{:S(2)}) collective-permute-start(bf16[2,128,512]{2,1,0:T(8,128)(2,1)S(1)} %bitcast.114), channel_id=1, source_target_pairs={{0,14},{2,16},{4,18},{6,20},{8,22},{10,24},{12,26},{14,28},{16,30}... | collective-permute-start | bytes 786440 | tf_op jit(solution)/shard_map/ppermute | solution.py:19
  198.2 23.6 %collective-permute-start.2 = (bf16[2,128,512]{2,1,0:T(8,128)(2,1)S(1)}, bf16[2,128,512]{2,1,0:T(8,128)(2,1)S(1)}, u32[]{:S(2)}, u32[]{:S(2)}) collective-permute-start(bf16[2,128,512]{2,1,0:T(8,128)(2,1)S(1)} %bitcast.115), channel_id=1, source_target_pairs={{0,12},{2,14},{4,16},{6,18},{8,20},{10,22},{12,24},{14,26},{16,28}... | collective-permute-start | bytes 786440 | tf_op jit(solution)/shard_map/ppermute | solution.py:19
  201.1 34.1 %collective-permute-start.3 = (bf16[2,128,512]{2,1,0:T(8,128)(2,1)S(1)}, bf16[2,128,512]{2,1,0:T(8,128)(2,1)S(1)}, u32[]{:S(2)}, u32[]{:S(2)}) collective-permute-start(bf16[2,128,512]{2,1,0:T(8,128)(2,1)S(1)} %bitcast.116), channel_id=1, source_target_pairs={{0,10},{2,12},{4,14},{6,16},{8,18},{10,20},{12,22},{14,24},{16,26}... | collective-permute-start | bytes 786440 | tf_op jit(solution)/shard_map/ppermute | solution.py:19
  203.1 40.8 %collective-permute-start.4 = (bf16[2,128,512]{2,1,0:T(8,128)(2,1)S(1)}, bf16[2,128,512]{2,1,0:T(8,128)(2,1)S(1)}, u32[]{:S(2)}, u32[]{:S(2)}) collective-permute-start(bf16[2,128,512]{2,1,0:T(8,128)(2,1)S(1)} %bitcast.117), channel_id=1, source_target_pairs={{0,8},{2,10},{4,12},{6,14},{8,16},{10,18},{12,20},{14,22},{16,24},... | collective-permute-start | bytes 786440 | tf_op jit(solution)/shard_map/ppermute | solution.py:19
  207.3 39.5 %collective-permute-start.5 = (bf16[2,128,512]{2,1,0:T(8,128)(2,1)S(1)}, bf16[2,128,512]{2,1,0:T(8,128)(2,1)S(1)}, u32[]{:S(2)}, u32[]{:S(2)}) collective-permute-start(bf16[2,128,512]{2,1,0:T(8,128)(2,1)S(1)} %bitcast.118), channel_id=1, source_target_pairs={{0,6},{2,8},{4,10},{6,12},{8,14},{10,16},{12,18},{14,20},{16,22},{... | collective-permute-start | bytes 786440 | tf_op jit(solution)/shard_map/ppermute | solution.py:19
  209.2 58.3 %collective-permute-start.6 = (bf16[2,128,512]{2,1,0:T(8,128)(2,1)S(1)}, bf16[2,128,512]{2,1,0:T(8,128)(2,1)S(1)}, u32[]{:S(2)}, u32[]{:S(2)}) collective-permute-start(bf16[2,128,512]{2,1,0:T(8,128)(2,1)S(1)} %bitcast.119), channel_id=1, source_target_pairs={{0,4},{2,6},{4,8},{6,10},{8,12},{10,14},{12,16},{14,18},{16,20},{1... | collective-permute-start | bytes 786440 | tf_op jit(solution)/shard_map/ppermute | solution.py:19
  221.8 48.0 %collective-permute-start.7 = (bf16[2,128,512]{2,1,0:T(8,128)(2,1)S(1)}, bf16[2,128,512]{2,1,0:T(8,128)(2,1)S(1)}, u32[]{:S(2)}, u32[]{:S(2)}) collective-permute-start(bf16[2,128,512]{2,1,0:T(8,128)(2,1)S(1)} %bitcast.120), channel_id=1, source_target_pairs={{0,2},{2,4},{4,6},{6,8},{8,10},{10,12},{12,14},{14,16},{16,18},{18... | collective-permute-start | bytes 786440 | tf_op jit(solution)/shard_map/ppermute | solution.py:19
Sparse Core Ops, SparseCore 0:
  10.7 38.8 all-gather.2
  56.8 103.4 all-reduce.1
  195.1 53.1 all-gather.4
where the time goes:
time: 290 us
  waiting for transfers between devices  172 us (59%)
  matrix products  42.2 us (15%)
  starting transfers between devices  41.2 us (14%)
  between operations  14.8 us (5%)
  blocking collectives  7 us (2%)
  other arithmetic  6.92 us (2%)
  local copies, waits for them, and re-layouts  5.59 us (2%)
    psum x1, waiting for transfers between devices, shards(): summed = lax.psum(partial_value, 'seq')  103 us
    ppermute x8, starting transfers between devices, from_behind(): return lax.ppermute(block, axis, route)  37.4 us
    ppermute x8, waiting for transfers between devices, from_behind(): return lax.ppermute(block, axis, route)  37.1 us
    all_gather x1, waiting for transfers between devices, shards(): lax.all_gather(old_low, 'seq', axis=1, tiled=True)  25.6 us
    dot_general x12, matrix products, gram_times(): return jnp.einsum('mij,mjk->mik', row_block, gram_matrix, precision=precise)  23.2 us
    all_to_all x1, blocking collectives, shards(): lax.all_to_all(combined, 'head', split_axis=0, concat_axis=1, tiled=True)  7 us
    all_to_all x1, waiting for transfers between devices, shards(): lax.all_to_all(qkv, 'head', split_axis=2, concat_axis=1, tiled=True)  6.67 us
    dot_general x5, matrix products, contract_last(): lax.dot_general(left_side, right_side, (((1,), (1,)), ((), ())), preferre...  5.86 us
  transfers between devices with their start and end apart: 12, of which 9 were waited for; matrix products, arithmetic and copies ran while one was open for 2% of the time, Pallas kernels for 0%

commit v1 on v0

--- a/solution.py
+++ b/solution.py
@@ -83,7 +83,7 @@
     partial_value = head_gradient(
         key_norm, signal, lax.all_gather(old_low, "seq", axis=1, tiled=True)
     )
-    summed = lax.psum(partial_value, "seq")
+    summed = jnp.sum(lax.all_gather(partial_value, "seq"), axis=0)
     frob_norm = jnp.sqrt(jnp.sum(summed * summed, axis=(1, 2), keepdims=True))
     normalized = summed / (frob_norm + norm_eps)
     gram_matrix = jnp.einsum("mij,mkj->mik", normalized, normalized, precision=precise)

time: 290 us -> 453 us (1.56)
  waiting for transfers between devices: 172 us -> 318 us
  other arithmetic: 6.92 us -> 26.2 us
    all_gather x0 -> x1, waiting for transfers between devices: none -> 246 us  [shards(): summed = jnp.sum(lax.all_gather(partial_value, 'seq'), axis=0)]
    psum x1 -> x0, waiting for transfers between devices: 103 us -> none  [shards(): summed = lax.psum(partial_value, 'seq')]
    reduce_sum x0 -> x1, other arithmetic: none -> 18.8 us  [shards(): summed = jnp.sum(lax.all_gather(partial_value, 'seq'), axis=0)]
where the time goes in v1:
time: 453 us; the launch traced here: 452 us
  waiting for transfers between devices  318 us (70%)
  matrix products  42.2 us (9%)
  starting transfers between devices  38.7 us (9%)
  other arithmetic  26.2 us (6%)
  between operations  14.9 us (3%)
  blocking collectives  7 us (2%)
  local copies, waits for them, and re-layouts  5.27 us (1%)
    all_gather x1, waiting for transfers between devices, shards(): summed = jnp.sum(lax.all_gather(partial_value, 'seq'), axis=0)  246 us
    ppermute x8, waiting for transfers between devices, from_behind(): return lax.ppermute(block, axis, route)  41.5 us
    ppermute x8, starting transfers between devices, from_behind(): return lax.ppermute(block, axis, route)  35.1 us
    all_gather x1, waiting for transfers between devices, shards(): lax.all_gather(old_low, 'seq', axis=1, tiled=True)  24.4 us
    dot_general x12, matrix products, gram_times(): return jnp.einsum('mij,mjk->mik', row_block, gram_matrix, precision=precise)  23.2 us
    reduce_sum x1, other arithmetic, shards(): summed = jnp.sum(lax.all_gather(partial_value, 'seq'), axis=0)  18.8 us
  transfers between devices with their start and end apart: 12, of which 9 were waited for; matrix products, arithmetic and copies ran while one was open for 2% of the time, Pallas kernels for 0%

profile of v1, /device:TPU:16, one launch (start us, length us, event | category | flops | bytes accessed | tf_op | source)
XLA Modules:
  0.0 452.5 jit_solution(9109874855339767129)
XLA Ops:
  11.9 3.5 all-to-all-start
  15.5 6.7 %all-to-all-done = bf16[2,2,49152]{2,1,0:T(2,128)(2,1)S(1)} async-done(((bf16[2,2,49152]{2,1,0:T(2,128)(2,1)}), bf16[2,2,49152]{2,1,0:T(2,128)(2,1)S(1)}, u32[]{:S(2)}, u32[]{:S(2)}) %all-to-all-start) | async-done | bytes 393248 | tf_op jit(solution)/shard_map/all_to_all | solution.py:73
  25.3 24.4 %all-gather.5.cloned.1.call-done = bf16[3,512,512]{2,1,0:T(8,128)(2,1)} async-done(((bf16[3,32,512]{2,1,0:T(8,128)(2,1)}), bf16[3,512,512]{2,1,0:T(8,128)(2,1)}) %all-gather.5.cloned.1.call-update) | async-done | bytes 1572880 | tf_op jit(solution)/shard_map/all_gather | solution.py:84
  54.7 1.9 pad_maximum_fusion
  58.8 245.6 %all-gather.9.cloned.1.call-done = f32[48,512,512]{2,1,0:T(8,128)} async-done(((f32[3,512,512]{2,1,0:T(8,128)}), f32[48,512,512]{2,1,0:T(8,128)}) %all-gather.9.cloned.1.call-update) | async-done | bytes 50331664 | tf_op jit(solution)/shard_map/all_gather | solution.py:86
  304.4 18.8 %reduce_sum.48 = f32[3,512,512]{2,1,0:T(8,128)S(1)} reduce(f32[16,3,512,512]{3,2,1,0:T(8,128)} %bitcast.106, f32[]{:T(128)} %constant.15.clone.1), dimensions={0}, to_apply=%region_4.5 | reduce | flops 11796480 | bytes 53477380 | tf_op jit(solution)/shard_map/reduce_sum | solution.py:86
  323.7 5.7 %fusion.15 = f32[3,512,512]{2,1,0:T(8,128)S(1)} fusion(f32[3,512,512]{2,1,0:T(8,128)S(1)} %reduce_sum.48, f32[3]{0:T(128)S(1)} %sqrt_add_fusion), kind=kOutput, calls=%fused_computation.33 | convolution fusion | flops 4832624640 | bytes 6291468 | tf_op jit(solution)/shard_map/mij,mkj->mik/dot_general | solution.py:89
  337.0 2.1 fusion.11
  350.5 2.1 fusion.6
  352.7 2.8 fusion.46
  356.8 3.2 collective-permute-start.1
  360.1 1.9 collective-permute-start.2
  362.0 1.9 collective-permute-start.3
  363.9 1.9 collective-permute-start.4
  365.9 2.8 collective-permute-done
  370.6 4.2 collective-permute-done.1
  374.8 10.0 %collective-permute-start.6 = (bf16[2,128,512]{2,1,0:T(8,128)(2,1)S(1)}, bf16[2,128,512]{2,1,0:T(8,128)(2,1)S(1)}, u32[]{:S(2)}, u32[]{:S(2)}) collective-permute-start(bf16[2,128,512]{2,1,0:T(8,128)(2,1)S(1)} %bitcast.121), channel_id=1, source_target_pairs={{0,4},{2,6},{4,8},{6,10},{8,12},{10,14},{12,16},{14,18},{16,20},{1... | collective-permute-start | bytes 786440 | tf_op jit(solution)/shard_map/ppermute | solution.py:19
  384.8 13.0 %collective-permute-start.7 = (bf16[2,128,512]{2,1,0:T(8,128)(2,1)S(1)}, bf16[2,128,512]{2,1,0:T(8,128)(2,1)S(1)}, u32[]{:S(2)}, u32[]{:S(2)}) collective-permute-start(bf16[2,128,512]{2,1,0:T(8,128)(2,1)S(1)} %bitcast.122), channel_id=1, source_target_pairs={{0,2},{2,4},{4,6},{6,8},{8,10},{10,12},{12,14},{14,16},{16,18},{18... | collective-permute-start | bytes 786440 | tf_op jit(solution)/shard_map/ppermute | solution.py:19
  397.9 9.4 %collective-permute-done.4 = bf16[2,128,512]{2,1,0:T(8,128)(2,1)S(1)} collective-permute-done((bf16[2,128,512]{2,1,0:T(8,128)(2,1)S(1)}, bf16[2,128,512]{2,1,0:T(8,128)(2,1)S(1)}, u32[]{:S(2)}, u32[]{:S(2)}) %collective-permute-start.4) | collective-permute-done | bytes 262176 | tf_op jit(solution)/shard_map/ppermute | solution.py:19
  407.3 2.7 collective-permute-done.5
  410.0 20.1 %collective-permute-done.6 = bf16[2,128,512]{2,1,0:T(8,128)(2,1)S(1)} collective-permute-done((bf16[2,128,512]{2,1,0:T(8,128)(2,1)S(1)}, bf16[2,128,512]{2,1,0:T(8,128)(2,1)S(1)}, u32[]{:S(2)}, u32[]{:S(2)}) %collective-permute-start.6) | collective-permute-done | bytes 262176 | tf_op jit(solution)/shard_map/ppermute | solution.py:19
  430.1 2.3 collective-permute-done.7
  434.6 2.4 fusion.14
  438.3 7.0 %all_to_all.34 = bf16[2,64,512]{2,1,0:T(8,128)(2,1)S(1)} all-to-all(bf16[2,64,512]{2,1,0:T(8,128)(2,1)S(1)} %bitcast.129), channel_id=1, replica_groups=mesh['seq'=16,'head'=2] {'head'}, dimensions={0} | all-to-all | bytes 262144 | tf_op jit(solution)/shard_map/all_to_all | solution.py:121
  (76 shorter events, 41.3 us)
Async XLA Ops:
  7.2 8.2 %copy-start.5 = (f32[128,1]{0,1:T(1,128)S(1)}, f32[128,1]{0,1:T(1,128)}, u32[]{:S(2)}) copy-start(f32[128,1]{0,1:T(1,128)} %param.5) | copy-start | bytes 1540
  7.2 42.5 %all-gather.5.cloned.1.call-start = ((), (), s32[]{:S(2)}) async-start(), calls=%async_computation.2 | async-start | bytes 1671168 | tf_op jit(solution)/shard_map/all_gather | solution.py:84
  11.9 10.3 %all-to-all-start = ((bf16[2,2,49152]{2,1,0:T(2,128)(2,1)}), bf16[2,2,49152]{2,1,0:T(2,128)(2,1)S(1)}, u32[]{:S(2)}, u32[]{:S(2)}) async-start(bf16[2,2,49152]{2,1,0:T(2,128)(2,1)} %reshape.125), calls=%async_computation | async-start | bytes 786432 | tf_op jit(solution)/shard_map/all_to_all | solution.py:73
  15.3 289.1 %all-gather.9.cloned.1.call-start = ((), (), s32[]{:S(2)}) async-start(), calls=%async_computation.4 | async-start | bytes 53477376 | tf_op jit(solution)/shard_map/all_gather | solution.py:86
  56.7 376.5 %all-gather.7.cloned.1.call-start = ((), (), s32[]{:S(2)}) async-start(), calls=%async_computation.3 | async-start | bytes 1671168 | tf_op jit(solution)/shard_map/all_gather | solution.py:100
  323.7 5.7 %copy-start.2 = (f32[32,512]{1,0:T(8,128)S(1)}, f32[32,512]{1,0:T(8,128)}, u32[]{:S(2)}) copy-start(f32[32,512]{1,0:T(8,128)} %fusion.37) | copy-start | bytes 196612
  342.9 3.8 copy-start.1
  348.6 4.1 copy-start.3
  355.4 77.1 %copy-start.4 = (bf16[1,2,64,512]{3,2,1,0:T(8,128)(2,1)S(1)}, bf16[1,2,64,512]{3,2,1,0:T(8,128)(2,1)}, u32[]{:S(2)}) copy-start(bf16[1,2,64,512]{3,2,1,0:T(8,128)(2,1)} %get-tuple-element.14) | copy-start | bytes 393220
  355.5 13.1 %collective-permute-start = (bf16[2,128,512]{2,1,0:T(8,128)(2,1)S(1)}, bf16[2,128,512]{2,1,0:T(8,128)(2,1)S(1)}, u32[]{:S(2)}, u32[]{:S(2)}) collective-permute-start(bf16[2,128,512]{2,1,0:T(8,128)(2,1)S(1)} %bitcast.115), channel_id=1, source_target_pairs={{0,16},{2,18},{4,20},{6,22},{8,24},{10,26},{12,28},{14,30},{1,17},... | collective-permute-start | bytes 786440 | tf_op jit(solution)/shard_map/ppermute | solution.py:19
  356.8 18.0 %collective-permute-start.1 = (bf16[2,128,512]{2,1,0:T(8,128)(2,1)S(1)}, bf16[2,128,512]{2,1,0:T(8,128)(2,1)S(1)}, u32[]{:S(2)}, u32[]{:S(2)}) collective-permute-start(bf16[2,128,512]{2,1,0:T(8,128)(2,1)S(1)} %bitcast.116), channel_id=1, source_target_pairs={{0,14},{2,16},{4,18},{6,20},{8,22},{10,24},{12,26},{14,28},{16,30}... | collective-permute-start | bytes 786440 | tf_op jit(solution)/shard_map/ppermute | solution.py:19
  360.1 24.7 %collective-permute-start.2 = (bf16[2,128,512]{2,1,0:T(8,128)(2,1)S(1)}, bf16[2,128,512]{2,1,0:T(8,128)(2,1)S(1)}, u32[]{:S(2)}, u32[]{:S(2)}) collective-permute-start(bf16[2,128,512]{2,1,0:T(8,128)(2,1)S(1)} %bitcast.117), channel_id=1, source_target_pairs={{0,12},{2,14},{4,16},{6,18},{8,20},{10,22},{12,24},{14,26},{16,28}... | collective-permute-start | bytes 786440 | tf_op jit(solution)/shard_map/ppermute | solution.py:19
  362.0 35.8 %collective-permute-start.3 = (bf16[2,128,512]{2,1,0:T(8,128)(2,1)S(1)}, bf16[2,128,512]{2,1,0:T(8,128)(2,1)S(1)}, u32[]{:S(2)}, u32[]{:S(2)}) collective-permute-start(bf16[2,128,512]{2,1,0:T(8,128)(2,1)S(1)} %bitcast.118), channel_id=1, source_target_pairs={{0,10},{2,12},{4,14},{6,16},{8,18},{10,20},{12,22},{14,24},{16,26}... | collective-permute-start | bytes 786440 | tf_op jit(solution)/shard_map/ppermute | solution.py:19
  363.9 43.3 %collective-permute-start.4 = (bf16[2,128,512]{2,1,0:T(8,128)(2,1)S(1)}, bf16[2,128,512]{2,1,0:T(8,128)(2,1)S(1)}, u32[]{:S(2)}, u32[]{:S(2)}) collective-permute-start(bf16[2,128,512]{2,1,0:T(8,128)(2,1)S(1)} %bitcast.119), channel_id=1, source_target_pairs={{0,8},{2,10},{4,12},{6,14},{8,16},{10,18},{12,20},{14,22},{16,24},... | collective-permute-start | bytes 786440 | tf_op jit(solution)/shard_map/ppermute | solution.py:19
  368.6 41.3 %collective-permute-start.5 = (bf16[2,128,512]{2,1,0:T(8,128)(2,1)S(1)}, bf16[2,128,512]{2,1,0:T(8,128)(2,1)S(1)}, u32[]{:S(2)}, u32[]{:S(2)}) collective-permute-start(bf16[2,128,512]{2,1,0:T(8,128)(2,1)S(1)} %bitcast.120), channel_id=1, source_target_pairs={{0,6},{2,8},{4,10},{6,12},{8,14},{10,16},{12,18},{14,20},{16,22},{... | collective-permute-start | bytes 786440 | tf_op jit(solution)/shard_map/ppermute | solution.py:19
  374.8 55.3 %collective-permute-start.6 = (bf16[2,128,512]{2,1,0:T(8,128)(2,1)S(1)}, bf16[2,128,512]{2,1,0:T(8,128)(2,1)S(1)}, u32[]{:S(2)}, u32[]{:S(2)}) collective-permute-start(bf16[2,128,512]{2,1,0:T(8,128)(2,1)S(1)} %bitcast.121), channel_id=1, source_target_pairs={{0,4},{2,6},{4,8},{6,10},{8,12},{10,14},{12,16},{14,18},{16,20},{1... | collective-permute-start | bytes 786440 | tf_op jit(solution)/shard_map/ppermute | solution.py:19
  384.8 47.6 %collective-permute-start.7 = (bf16[2,128,512]{2,1,0:T(8,128)(2,1)S(1)}, bf16[2,128,512]{2,1,0:T(8,128)(2,1)S(1)}, u32[]{:S(2)}, u32[]{:S(2)}) collective-permute-start(bf16[2,128,512]{2,1,0:T(8,128)(2,1)S(1)} %bitcast.122), channel_id=1, source_target_pairs={{0,2},{2,4},{4,6},{6,8},{8,10},{10,12},{12,14},{14,16},{16,18},{18... | collective-permute-start | bytes 786440 | tf_op jit(solution)/shard_map/ppermute | solution.py:19
  397.9 35.3 %copy-start = (bf16[1,2,64,512]{3,2,1,0:T(8,128)(2,1)S(1)}, bf16[1,2,64,512]{3,2,1,0:T(8,128)(2,1)}, u32[]{:S(2)}) copy-start(bf16[1,2,64,512]{3,2,1,0:T(8,128)(2,1)} %get-tuple-element.18) | copy-start | bytes 393220
Sparse Core Ops, SparseCore 0:
  10.7 38.8 all-gather.4
  56.8 247.6 all-gather.8
  355.6 52.1 all-gather.6
